TPU v7x, 32 devices: a whole 2x2x4 slice. The times are simulated.
32 devices in a mesh: pulse: 4 (over z), tile: 8 (over y, x, core).
Axes of the slice: x: 2, y: 2, z: 4, core: 2. Of those that a mesh axis runs over, the one named last changes fastest.
Arguments:
- raw: bfloat16 [2, 128, 2048], P(None, ('pulse', 'tile')), may hold values from -6 to 6
- filt: bfloat16 [2, 1024, 2048], replicated, may hold values from -0.125 to 0.125
- range_off: int32 [128], P(('pulse', 'tile')), may hold values from 0 to 1024
- fine: int32 [128], P(('pulse', 'tile')), may hold values from 0 to 3
- dop: int32 [128], P(('pulse', 'tile')), may hold values from 0 to 511
- pulse_order: int32 [32, 4], P(('pulse', 'tile')), may hold values from 0 to 3, each once within a row
- band_idx: int32 [8, 128], P(None, ('pulse', 'tile')), may hold values from 0 to 1023
Outputs:
- image: bfloat16 [2, 512, 32768], P(None, 'pulse', 'tile')
Inputs may be any that keep to these rules, and one draw needn't show every extreme that they name: `pulse_order`: each row is a permutation of 0 .. 3.
All inputs are finite; a program needn't handle non-finite values.
Results may differ from a plain program's by a relative error of at most 0.0065.
Values may be sent and summed in bfloat16 or wider, within the bound.
A program may use at most 192 MiB of HBM per device.

v0:
```python
import jax
import jax.numpy as jnp
from jax import lax
from jax.sharding import PartitionSpec as P

BAND = 1024
STEPS = 4
PS = 1
R_DEV = 128


def compress(windows, filt):
    wr = windows[:, 0]
    wi = windows[:, 1]
    prof_re = jnp.dot(wr, filt[0], preferred_element_type=jnp.float32) - jnp.dot(
        wi, filt[1], preferred_element_type=jnp.float32
    )
    prof_im = jnp.dot(wr, filt[1], preferred_element_type=jnp.float32) + jnp.dot(
        wi, filt[0], preferred_element_type=jnp.float32
    )
    return jnp.stack([prof_re, prof_im], 1).astype(jnp.bfloat16)


def cut_band(profile, start):
    segment = lax.dynamic_slice_in_dim(profile, start, BAND + 1, 1)
    return (segment[:, :BAND], segment[:, BAND])


def interpolate(pieces, edges, shifts):
    first = pieces.astype(jnp.float32)
    second = jnp.concatenate([first[..., 1:], edges.astype(jnp.float32)[..., None]], -1)
    first = jnp.repeat(first, 4, axis=-1)
    second = jnp.repeat(second, 4, axis=-1)
    phase_q = (jnp.arange(4 * BAND, dtype=jnp.int32) % 4).astype(jnp.float32)
    weight = (4.0 * phase_q[None, :] + shifts.astype(jnp.float32)[:, None]) / 16.0
    weight = weight[:, None, :]
    return first * (1.0 - weight) + second * weight


def gradient_terms(samples, summed):
    sr = samples[:, 0]
    si = samples[:, 1]
    g_re = jnp.sum(sr * summed[None, 0] + si * summed[None, 1], axis=-1)
    g_im = jnp.sum(si * summed[None, 0] - sr * summed[None, 1], axis=-1)
    return (g_re, g_im)


def shards(raw, filt, range_off, fine, dop, pulse_order, band_idx):
    n_pulse = lax.axis_size("pulse")
    n_tile = lax.axis_size("tile")
    devices = n_pulse * n_tile
    pulse_index = lax.axis_index("pulse")
    p_dev = raw.shape[1]
    win = filt.shape[1]
    pulses = p_dev * devices
    total_rows = R_DEV * n_pulse
    cols = 4 * BAND
    all_order, all_dop, all_fine = (
        lax.all_gather(pulse_order, ("pulse", "tile"), axis=0, tiled=True),
        lax.all_gather(dop, ("pulse", "tile"), axis=0, tiled=True),
        lax.all_gather(fine, ("pulse", "tile"), axis=0, tiled=True),
    )
    owners = jnp.arange(devices, dtype=jnp.int32)[:, None] * p_dev
    rows_here = pulse_index * R_DEV + jnp.arange(R_DEV, dtype=jnp.int32)
    accumulated = jnp.zeros((2, R_DEV, cols), jnp.float32)
    for step in range(STEPS):
        local_sel = pulse_order[0, step * PS : (step + 1) * PS]
        picked = jnp.take(raw, local_sel, axis=1)
        offsets = jnp.take(range_off, local_sel)
        windows = jax.vmap(
            lambda row, off: lax.dynamic_slice_in_dim(row, off, win, 1), in_axes=(1, 0)
        )(picked, offsets)
        profile = compress(windows, filt)
        chosen = (owners + all_order[:, step * PS : (step + 1) * PS]).reshape(-1)
        starts = jnp.take(band_idx, local_sel, axis=1)
        pieces, edges = jax.vmap(jax.vmap(cut_band, in_axes=(0, 0)), in_axes=(None, 0))(
            profile, starts
        )
        pieces = pieces.reshape(n_tile * PS, 2, BAND)
        edges = edges.reshape(n_tile * PS, 2)
        mine_pieces, mine_edges = (
            lax.all_to_all(pieces, "tile", split_axis=0, concat_axis=0, tiled=True),
            lax.all_to_all(edges, "tile", split_axis=0, concat_axis=0, tiled=True),
        )
        pieces, edges = (
            lax.all_gather(mine_pieces, "pulse", axis=0, tiled=True),
            lax.all_gather(mine_edges, "pulse", axis=0, tiled=True),
        )
        shifts = jnp.take(all_fine, chosen)
        samples = interpolate(pieces, edges, shifts)
        summed = jnp.sum(samples, axis=0)
        g_re, g_im = gradient_terms(samples, summed)
        g_re, g_im = lax.psum((g_re, g_im), "tile")
        scale = jnp.sqrt(g_re * g_re + g_im * g_im + 1.0)
        c_re = (g_re / scale)[:, None]
        c_im = (-g_im / scale)[:, None]
        sr = samples[:, 0]
        si = samples[:, 1]
        right = jnp.concatenate([c_re * sr - c_im * si, c_re * si + c_im * sr], 0).astype(
            jnp.bfloat16
        )
        dops = jnp.take(all_dop, chosen)
        angle = (
            2.0
            * jnp.pi
            * (dops[:, None] * rows_here[None, :] % total_rows).astype(jnp.float32)
            / total_rows
        )
        norm_scale = jnp.sqrt(jnp.float32(pulses))
        e_re = (jnp.cos(angle) / norm_scale).astype(jnp.bfloat16)
        e_im = (jnp.sin(angle) / norm_scale).astype(jnp.bfloat16)
        left = jnp.stack([jnp.concatenate([e_re, -e_im], 0), jnp.concatenate([e_im, e_re], 0)], 0)
        accumulated = accumulated + jnp.einsum(
            "zkr,kc->zrc", left, right, preferred_element_type=jnp.float32
        )
    return accumulated.astype(jnp.bfloat16)


def solution(mesh):
    return jax.shard_map(
        shards,
        mesh=mesh,
        in_specs=(
            P(None, ("pulse", "tile"), None),
            P(),
            P(("pulse", "tile")),
            P(("pulse", "tile")),
            P(("pulse", "tile")),
            P(("pulse", "tile"), None),
            P(None, ("pulse", "tile")),
        ),
        out_specs=P(None, "pulse", "tile"),
        check_vma=False,
    )
```

profile of v0, /device:TPU:0, one launch (start us, length us, event | category | flops | bytes accessed | tf_op | source)
XLA Modules:
  0.0 478.1 jit_solution(11086329522314578801)
XLA Ops:
  21.8 10.7 %while.17 = (s32[]{:T(128)}, bf16[1,2,2048]{2,1,0:T(2,128)(2,1)S(1)}, s32[8,3]{0,1:T(4,128)S(1)}, bf16[8,2,1025]{2,1,0:T(2,128)(2,1)S(1)}, s32[]{:T(128)}) while((s32[]{:T(128)}, bf16[1,2,2048]{2,1,0:T(2,128)(2,1)S(1)}, s32[8,3]{0,1:T(4,128)S(1)}, bf16[8,2,1025]{2,1,0:T(2,128)(2,1)S(1)}, s32[]{:T(128)}) %tuple.191), condition=%wide.while_cond.13, body=%wide.while_body.13.sunk | while | flops 2 | bytes 9321 | solution.py:25
  33.3 5.2 %all-to-all-start.7 = ((bf16[8,1,2]{2,1,0:T(2,128)(2,1)}), bf16[8,1,2]{2,1,0:T(2,128)(2,1)S(1)}, u32[]{:S(2)}, u32[]{:S(2)}) async-start(bf16[8,1,2]{2,1,0:T(2,128)(2,1)} %copy.117), calls=%async_computation.7 | async-start | bytes 8192 | tf_op jit(solution)/shard_map/all_to_all | solution.py:83
  39.1 42.3 %all-gather.4 = s32[32,1,4]{2,1,0:T(1,128)S(1)} all-gather(s32[1,1,4]{2,1,0:T(1,128)S(1)} %bitcast.332), channel_id=1, replica_groups=mesh['pulse'=4,'tile'=8] {'pulse','tile'}, dimensions={0}, use_global_device_ids=true | all-gather | bytes 528 | tf_op jit(solution)/shard_map/all_gather | solution.py:59
  82.0 37.2 %all-reduce.6 = (s32[128]{0:T(128)S(1)}, s32[128]{0:T(128)S(1)}) all-reduce(s32[128]{0:T(128)S(1)} %dynamic-update-slice.19, s32[128]{0:T(128)S(1)} %dynamic-update-slice.18), channel_id=1, replica_groups=mesh['pulse'=4,'tile'=8] {'pulse','tile'}, use_global_device_ids=true, to_apply=%add.5 | all-reduce | flops 256 | bytes 2048
  136.4 10.9 %while.16 = (s32[]{:T(128)}, bf16[1,2,2048]{2,1,0:T(2,128)(2,1)S(1)}, s32[8,3]{0,1:T(4,128)S(1)}, bf16[8,2,1025]{2,1,0:T(2,128)(2,1)S(1)}, s32[]{:T(128)}) while((s32[]{:T(128)}, bf16[1,2,2048]{2,1,0:T(2,128)(2,1)S(1)}, s32[8,3]{0,1:T(4,128)S(1)}, bf16[8,2,1025]{2,1,0:T(2,128)(2,1)S(1)}, s32[]{:T(128)}) %tuple.188), condition=%wide.while_cond.10, body=%wide.while_body.10.sunk | while | flops 2 | bytes 9321 | solution.py:25
  159.4 11.5 %while.15 = (s32[]{:T(128)}, bf16[1,2,2048]{2,1,0:T(2,128)(2,1)S(1)}, s32[8,3]{0,1:T(4,128)S(1)}, bf16[8,2,1025]{2,1,0:T(2,128)(2,1)S(1)}, s32[]{:T(128)}) while((s32[]{:T(128)}, bf16[1,2,2048]{2,1,0:T(2,128)(2,1)S(1)}, s32[8,3]{0,1:T(4,128)S(1)}, bf16[8,2,1025]{2,1,0:T(2,128)(2,1)S(1)}, s32[]{:T(128)}) %tuple.185), condition=%wide.while_cond.7, body=%wide.while_body.7.sunk | while | flops 2 | bytes 9321 | solution.py:25
  183.1 11.3 %while.14 = (s32[]{:T(128)}, bf16[1,2,2048]{2,1,0:T(2,128)(2,1)S(1)}, s32[8,3]{0,1:T(4,128)S(1)}, bf16[8,2,1025]{2,1,0:T(2,128)(2,1)S(1)}, s32[]{:T(128)}) while((s32[]{:T(128)}, bf16[1,2,2048]{2,1,0:T(2,128)(2,1)S(1)}, s32[8,3]{0,1:T(4,128)S(1)}, bf16[8,2,1025]{2,1,0:T(2,128)(2,1)S(1)}, s32[]{:T(128)}) %tuple.182), condition=%wide.while_cond.4, body=%wide.while_body.4.sunk | while | flops 2 | bytes 9321 | solution.py:25
  219.4 15.0 %all-to-all-start.5 = ((bf16[8,1,2]{2,1,0:T(2,128)(2,1)}), bf16[8,1,2]{2,1,0:T(2,128)(2,1)S(1)}, u32[]{:S(2)}, u32[]{:S(2)}) async-start(bf16[8,1,2]{2,1,0:T(2,128)(2,1)} %copy.107), calls=%async_computation.5 | async-start | bytes 8192 | tf_op jit(solution)/shard_map/all_to_all | solution.py:83
  234.4 13.8 %all-gather.3 = bf16[32,1,2]{2,1,0:T(2,128)(2,1)S(1)} all-gather(bf16[8,1,2]{2,1,0:T(2,128)(2,1)S(1)} %all-to-all-done.7), channel_id=5, replica_groups=mesh['pulse'=4,'tile'=8] {'pulse'}, dimensions={0}, use_global_device_ids=true | all-gather | bytes 160 | tf_op jit(solution)/shard_map/all_gather | solution.py:87
  248.3 4.1 all-to-all-start.3
  252.4 13.2 %all-gather.2 = bf16[32,1,2]{2,1,0:T(2,128)(2,1)S(1)} all-gather(bf16[8,1,2]{2,1,0:T(2,128)(2,1)S(1)} %all-to-all-done.5), channel_id=4, replica_groups=mesh['pulse'=4,'tile'=8] {'pulse'}, dimensions={0}, use_global_device_ids=true | all-gather | bytes 160 | tf_op jit(solution)/shard_map/all_gather | solution.py:87
  265.7 4.2 all-to-all-start.1
  269.9 13.2 %all-gather.1 = bf16[32,1,2]{2,1,0:T(2,128)(2,1)S(1)} all-gather(bf16[8,1,2]{2,1,0:T(2,128)(2,1)S(1)} %all-to-all-done.3), channel_id=3, replica_groups=mesh['pulse'=4,'tile'=8] {'pulse'}, dimensions={0}, use_global_device_ids=true | all-gather | bytes 160 | tf_op jit(solution)/shard_map/all_gather | solution.py:87
  283.2 4.2 all-to-all-start.6
  287.4 13.2 %all-gather = bf16[32,1,2]{2,1,0:T(2,128)(2,1)S(1)} all-gather(bf16[8,1,2]{2,1,0:T(2,128)(2,1)S(1)} %all-to-all-done.1), channel_id=2, replica_groups=mesh['pulse'=4,'tile'=8] {'pulse'}, dimensions={0}, use_global_device_ids=true | all-gather | bytes 160 | tf_op jit(solution)/shard_map/all_gather | solution.py:87
  301.1 4.2 all-to-all-start.4
  305.3 13.4 %all_gather.42 = bf16[32,2,1024]{2,1,0:T(2,128)(2,1)S(1)} all-gather(bf16[8,2,1024]{2,1,0:T(2,128)(2,1)S(1)} %all-to-all-done.6), channel_id=1, replica_groups=mesh['pulse'=4,'tile'=8] {'pulse'}, dimensions={0}, use_global_device_ids=true | all-gather | bytes 163840 | tf_op jit(solution)/shard_map/all_gather | solution.py:86
  320.1 4.2 all-to-all-start.2
  324.3 13.4 %all_gather.40 = bf16[32,2,1024]{2,1,0:T(2,128)(2,1)S(1)} all-gather(bf16[8,2,1024]{2,1,0:T(2,128)(2,1)S(1)} %all-to-all-done.4), channel_id=1, replica_groups=mesh['pulse'=4,'tile'=8] {'pulse'}, dimensions={0}, use_global_device_ids=true | all-gather | bytes 163840 | tf_op jit(solution)/shard_map/all_gather | solution.py:86
  339.8 4.2 all-to-all-start
  344.0 13.4 %all_gather.38 = bf16[32,2,1024]{2,1,0:T(2,128)(2,1)S(1)} all-gather(bf16[8,2,1024]{2,1,0:T(2,128)(2,1)S(1)} %all-to-all-done.2), channel_id=1, replica_groups=mesh['pulse'=4,'tile'=8] {'pulse'}, dimensions={0}, use_global_device_ids=true | all-gather | bytes 163840 | tf_op jit(solution)/shard_map/all_gather | solution.py:86
  358.5 13.6 %all_gather.35 = bf16[32,2,1024]{2,1,0:T(2,128)(2,1)S(1)} all-gather(bf16[8,2,1024]{2,1,0:T(2,128)(2,1)S(1)} %all-to-all-done), channel_id=1, replica_groups=mesh['pulse'=4,'tile'=8] {'pulse'}, dimensions={0}, use_global_device_ids=true | all-gather | bytes 163840 | tf_op jit(solution)/shard_map/all_gather | solution.py:86
  376.4 3.6 copy.121
  380.0 3.9 broadcast_in_dim.159
  387.6 5.1 %add_reduce_fusion = f32[2,1024,4]{2,1,0:T(8,128)S(1)} fusion(f32[32,1024,4]{0,2,1:T(4,128)} %copy.123, f32[32,1024,4]{0,2,1:T(4,128)} %copy.122, f32[32,2,1024]{0,2,1:T(8,128)S(1)} %copy.120, f32[32,2,1024]{0,2,1:T(8,128)} %copy.114), kind=kLoop, calls=%fused_computation.52 | loop fusion | flops 1040384 | bytes 1605632 | tf_op jit(solution)/shard_map/reduce_sum | solution.py:91
  398.6 3.6 copy.111
  402.3 3.9 broadcast_in_dim.152
  409.8 5.1 %add_reduce_fusion.1 = f32[2,1024,4]{2,1,0:T(8,128)S(1)} fusion(f32[32,1024,4]{0,2,1:T(4,128)} %copy.113, f32[32,1024,4]{0,2,1:T(4,128)} %copy.112, f32[32,2,1024]{0,2,1:T(8,128)S(1)} %copy.110, f32[32,2,1024]{0,2,1:T(8,128)} %copy.104), kind=kLoop, calls=%fused_computation.53 | loop fusion | flops 1040384 | bytes 1605632 | tf_op jit(solution)/shard_map/reduce_sum | solution.py:91
  429.6 5.1 %add_reduce_fusion.2 = f32[2,1024,4]{2,1,0:T(8,128)S(1)} fusion(f32[32,1024,4]{0,2,1:T(4,128)} %copy.103, f32[32,1024,4]{0,2,1:T(4,128)} %copy.102, f32[32,2,1024]{0,2,1:T(8,128)S(1)} %copy.100, f32[32,2,1024]{0,2,1:T(8,128)S(1)} %copy.94), kind=kLoop, calls=%fused_computation.54 | loop fusion | flops 1040384 | bytes 1605632 | tf_op jit(solution)/shard_map/reduce_sum | solution.py:91
  435.9 5.0 %add_reduce_fusion.3 = f32[2,1024,4]{2,1,0:T(8,128)S(1)} fusion(f32[32,1024,4]{0,2,1:T(4,128)} %copy.93, f32[32,1024,4]{0,2,1:T(4,128)} %copy.92, f32[32,2,1024]{0,2,1:T(8,128)S(1)} %copy.90, f32[32,2,1024]{0,2,1:T(8,128)S(1)} %copy.84), kind=kLoop, calls=%fused_computation.55 | loop fusion | flops 1040384 | bytes 1605632 | tf_op jit(solution)/shard_map/reduce_sum | solution.py:91
  450.5 3.7 copy.85
  459.4 12.1 %all-reduce.7 = (f32[32]{0:T(128)S(1)}, f32[32]{0:T(128)S(1)}, f32[32]{0:T(128)S(1)}, f32[32]{0:T(128)S(1)}, f32[32]{0:T(128)S(1)}, /*index=5*/f32[32]{0:T(128)S(1)}, f32[32]{0:T(128)S(1)}, f32[32]{0:T(128)S(1)}) all-reduce(f32[32]{0:T(128)S(1)} %get-tuple-element.157, ...), channel_id=1, replica_groups=mesh['pulse'=4,'tile'=8] {'tile'}, use_global_device_ids=true, to_apply=%region_4.8 | all-reduce | flops 256 | bytes 2048 | tf_op jit(solution)/shard_map/psum | solution.py:93
  (334 shorter events, 184.0 us)
Async XLA Ops:
  13.9 6.3 %copy-start = (bf16[2,1024,2048]{2,1,0:T(8,128)(2,1)S(1)}, bf16[2,1024,2048]{2,1,0:T(8,128)(2,1)}, u32[]{:S(2)}) copy-start(bf16[2,1024,2048]{2,1,0:T(8,128)(2,1)} %param.14) | copy-start | bytes 25165828
  20.3 18.9 %copy-start.24 = (s32[1,4]{1,0:T(1,128)S(1)}, s32[1,4]{1,0:T(1,128)}, u32[]{:S(2)}) copy-start(s32[1,4]{1,0:T(1,128)} %param.18) | copy-start | bytes 52
  20.3 61.2 %copy-start.26 = (s32[4]{0:T(128)S(1)}, s32[4]{0:T(128)}, u32[]{:S(2)}) copy-start(s32[4]{0:T(128)} %param.17) | copy-start | bytes 52
  20.3 61.5 %copy-start.27 = (s32[4]{0:T(128)S(1)}, s32[4]{0:T(128)}, u32[]{:S(2)}) copy-start(s32[4]{0:T(128)} %param.16) | copy-start | bytes 52
  33.3 186.1 %all-to-all-start.7 = ((bf16[8,1,2]{2,1,0:T(2,128)(2,1)}), bf16[8,1,2]{2,1,0:T(2,128)(2,1)S(1)}, u32[]{:S(2)}, u32[]{:S(2)}) async-start(bf16[8,1,2]{2,1,0:T(2,128)(2,1)} %copy.117), calls=%async_computation.7 | async-start | bytes 8192 | tf_op jit(solution)/shard_map/all_to_all | solution.py:83
  219.4 28.9 %all-to-all-start.5 = ((bf16[8,1,2]{2,1,0:T(2,128)(2,1)}), bf16[8,1,2]{2,1,0:T(2,128)(2,1)S(1)}, u32[]{:S(2)}, u32[]{:S(2)}) async-start(bf16[8,1,2]{2,1,0:T(2,128)(2,1)} %copy.107), calls=%async_computation.5 | async-start | bytes 8192 | tf_op jit(solution)/shard_map/all_to_all | solution.py:83
  248.3 17.4 %all-to-all-start.3 = ((bf16[8,1,2]{2,1,0:T(2,128)(2,1)}), bf16[8,1,2]{2,1,0:T(2,128)(2,1)S(1)}, u32[]{:S(2)}, u32[]{:S(2)}) async-start(bf16[8,1,2]{2,1,0:T(2,128)(2,1)} %copy.97), calls=%async_computation.3 | async-start | bytes 8192 | tf_op jit(solution)/shard_map/all_to_all | solution.py:83
  265.7 17.5 %all-to-all-start.1 = ((bf16[8,1,2]{2,1,0:T(2,128)(2,1)}), bf16[8,1,2]{2,1,0:T(2,128)(2,1)S(1)}, u32[]{:S(2)}, u32[]{:S(2)}) async-start(bf16[8,1,2]{2,1,0:T(2,128)(2,1)} %copy.87), calls=%async_computation.1 | async-start | bytes 8192 | tf_op jit(solution)/shard_map/all_to_all | solution.py:83
  283.2 17.9 %all-to-all-start.6 = ((bf16[8,2,1024]{2,1,0:T(2,128)(2,1)}), bf16[8,2,1024]{2,1,0:T(2,128)(2,1)S(1)}, u32[]{:S(2)}, u32[]{:S(2)}) async-start(bf16[8,2,1024]{2,1,0:T(2,128)(2,1)} %slice_bitcast_fusion.8), calls=%async_computation.6 | async-start | bytes 65536 | tf_op jit(solution)/shard_map/all_to_all | solution.py:82
  301.1 19.0 %all-to-all-start.4 = ((bf16[8,2,1024]{2,1,0:T(2,128)(2,1)}), bf16[8,2,1024]{2,1,0:T(2,128)(2,1)S(1)}, u32[]{:S(2)}, u32[]{:S(2)}) async-start(bf16[8,2,1024]{2,1,0:T(2,128)(2,1)} %slice_bitcast_fusion.9), calls=%async_computation.4 | async-start | bytes 65536 | tf_op jit(solution)/shard_map/all_to_all | solution.py:82
  320.1 19.7 %all-to-all-start.2 = ((bf16[8,2,1024]{2,1,0:T(2,128)(2,1)}), bf16[8,2,1024]{2,1,0:T(2,128)(2,1)S(1)}, u32[]{:S(2)}, u32[]{:S(2)}) async-start(bf16[8,2,1024]{2,1,0:T(2,128)(2,1)} %slice_bitcast_fusion.10), calls=%async_computation.2 | async-start | bytes 65536 | tf_op jit(solution)/shard_map/all_to_all | solution.py:82
  339.8 18.6 %all-to-all-start = ((bf16[8,2,1024]{2,1,0:T(2,128)(2,1)}), bf16[8,2,1024]{2,1,0:T(2,128)(2,1)S(1)}, u32[]{:S(2)}, u32[]{:S(2)}) async-start(bf16[8,2,1024]{2,1,0:T(2,128)(2,1)} %slice_bitcast_fusion.11), calls=%async_computation | async-start | bytes 65536 | tf_op jit(solution)/shard_map/all_to_all | solution.py:82
  429.6 5.8 %copy-start.16 = (f32[32,2,1023]{2,1,0:T(2,128)S(1)}, f32[32,2,1023]{2,1,0:T(2,128)}, u32[]{:S(2)}) copy-start(f32[32,2,1023]{2,1,0:T(2,128)} %slice.397) | copy-start | bytes 785668
  447.7 6.4 %copy-start.2 = (f32[32,2,4096]{2,0,1:T(8,128)S(1)}, f32[32,2,4096]{2,0,1:T(8,128)}, u32[]{:S(2)}) copy-start(f32[32,2,4096]{2,0,1:T(8,128)} %copy.121) | copy-start | bytes 3145732
  447.8 6.4 %copy-start.3 = (f32[32,2,4096]{2,0,1:T(8,128)S(1)}, f32[32,2,4096]{2,0,1:T(8,128)}, u32[]{:S(2)}) copy-start(f32[32,2,4096]{2,0,1:T(8,128)} %copy.115) | copy-start | bytes 3145732
  450.4 5.3 %copy-start.22 = (f32[4096]{0:T(1024)S(1)}, f32[4096]{0:T(1024)}, u32[]{:S(2)}) copy-start(f32[4096]{0:T(1024)} %mul.561) | copy-start | bytes 49156
  450.5 5.3 %copy-start.23 = (f32[4096]{0:T(1024)S(1)}, f32[4096]{0:T(1024)}, u32[]{:S(2)}) copy-start(f32[4096]{0:T(1024)} %mul.564) | copy-start | bytes 49156
  450.5 5.6 %copy-start.4 = (f32[32,2,4096]{2,0,1:T(8,128)S(1)}, f32[32,2,4096]{2,0,1:T(8,128)}, u32[]{:S(2)}) copy-start(f32[32,2,4096]{2,0,1:T(8,128)} %copy.111) | copy-start | bytes 3145732
  454.2 1.9 copy-start.5
  454.2 1.9 copy-start.14
  454.2 1.9 copy-start.15
  455.7 2.4 copy-start.1
  455.7 1.7 copy-start.6
  455.7 2.0 copy-start.7
  455.8 2.1 copy-start.12
  455.8 2.2 copy-start.13
  456.3 2.1 copy-start.8
  456.3 2.3 copy-start.9
  456.3 2.4 copy-start.10
  456.4 2.6 copy-start.11
  459.1 14.4 %copy-start.20 = (bf16[1,64,128]{2,1,0:T(8,128)(2,1)S(1)}, bf16[1,64,128]{2,1,0:T(8,128)(2,1)}, u32[]{:S(2)}) copy-start(bf16[1,64,128]{2,1,0:T(8,128)(2,1)} %get-tuple-element.254) | copy-start | bytes 49156
  459.1 14.4 %copy-start.21 = (bf16[1,64,128]{2,1,0:T(8,128)(2,1)S(1)}, bf16[1,64,128]{2,1,0:T(8,128)(2,1)}, u32[]{:S(2)}) copy-start(bf16[1,64,128]{2,1,0:T(8,128)(2,1)} %get-tuple-element.255) | copy-start | bytes 49156
  (4 other events, 4.6 us)
where the time goes:
time: 484 us; the launch traced here: 478 us
  blocking collectives  199 us (41%)
  local copies, waits for them, and re-layouts  142 us (29%)
  matrix products  46 us (10%)
  starting transfers between devices  45.2 us (9%)
  other arithmetic  35.4 us (7%)
  between operations  11 us (2%)
    all_gather x4, blocking collectives, shards(): lax.all_gather(mine_pieces, 'pulse', axis=0, tiled=True)  53.7 us
    all_gather x4, blocking collectives, shards(): lax.all_gather(mine_edges, 'pulse', axis=0, tiled=True)  53.4 us
    gather x96, local copies, waits for them, and re-layouts  44.3 us
    all_gather x1, blocking collectives, shards(): lax.all_gather(pulse_order, ('pulse', 'tile'), axis=0, tiled=True)  42.3 us
    unnamed x1, blocking collectives  37.2 us
    all_to_all x4, starting transfers between devices, shards(): lax.all_to_all(edges, 'tile', split_axis=0, concat_axis=0, tiled=True)  28.5 us
    reduce_sum x4, other arithmetic, shards(): summed = jnp.sum(samples, axis=0)  20.3 us
    all_to_all x4, starting transfers between devices, shards(): lax.all_to_all(pieces, 'tile', split_axis=0, concat_axis=0, tiled=True)  16.7 us
  transfers between devices with their start and end apart: 8, of which 0 were waited for; matrix products, arithmetic and copies ran while one was open for 22% of the time, Pallas kernels for 0%

commit v1 on v0

--- a/solution.py
+++ b/solution.py
@@ -7,6 +7,18 @@
 STEPS = 4
 PS = 1
 R_DEV = 128
+
+
+def gather_by_bits(array, axis, dim):
+    ways, here = (lax.axis_size(axis), lax.axis_index(axis))
+    grown, reach = (array, 1)
+    while reach < ways:
+        theirs = lax.ppermute(grown, axis, [(d, d ^ reach) for d in range(ways)])
+        mine_first = jnp.concatenate([grown, theirs], axis=dim)
+        theirs_first = jnp.concatenate([theirs, grown], axis=dim)
+        grown = jnp.where(here & reach == 0, mine_first, theirs_first)
+        reach = 2 * reach
+    return grown
 
 
 def compress(windows, filt):
@@ -83,7 +95,7 @@
             lax.all_to_all(edges, "tile", split_axis=0, concat_axis=0, tiled=True),
         )
         pieces, edges = (
-            lax.all_gather(mine_pieces, "pulse", axis=0, tiled=True),
+            gather_by_bits(mine_pieces, "pulse", 0),
             lax.all_gather(mine_edges, "pulse", axis=0, tiled=True),
         )
         shifts = jnp.take(all_fine, chosen)

time: 484 us -> 449 us (0.928)
  blocking collectives: 199 us -> 161 us
  starting transfers between devices: 45.2 us -> 34.8 us
  waiting for transfers between devices: 0.02 us -> 5.92 us
    all_gather x4 -> x0, blocking collectives: 53.7 us -> none  [shards(): lax.all_gather(mine_pieces, 'pulse', axis=0, tiled=True)]
    all_to_all x4 -> x2, starting transfers between devices: 28.5 us -> 8.75 us  [shards(): lax.all_to_all(edges, 'tile', split_axis=0, concat_axis=0, tiled=True)]
    all_to_all x0 -> x2, blocking collectives: none -> 15.7 us  [shards(): lax.all_to_all(edges, 'tile', split_axis=0, concat_axis=0, tiled=True)]
    ppermute x0 -> x8, starting transfers between devices: none -> 10.2 us  [gather_by_bits(): theirs = lax.ppermute(grown, axis, [(d, d ^ reach) for d in range(ways)])]
  transfers between devices with their start and end apart: 8 -> 14, of which waited for: 0 -> 2; matrix products, arithmetic and copies ran while one was open for 22% -> 24% of each run, Pallas kernels for 0% -> 0%
where the time goes in v1:
time: 449 us; the launch traced here: 443 us
  blocking collectives  161 us (36%)
  local copies, waits for them, and re-layouts  146 us (33%)
  matrix products  46 us (10%)
  other arithmetic  38.6 us (9%)
  starting transfers between devices  34.8 us (8%)
  between operations  11.1 us (2%)
  waiting for transfers between devices  5.92 us (1%)
    all_gather x4, blocking collectives, shards(): lax.all_gather(mine_edges, 'pulse', axis=0, tiled=True)  53.4 us
    gather x96, local copies, waits for them, and re-layouts  44 us
    all_gather x1, blocking collectives, shards(): lax.all_gather(pulse_order, ('pulse', 'tile'), axis=0, tiled=True)  42.3 us
    unnamed x1, blocking collectives  37.3 us
    reduce_sum x4, other arithmetic, shards(): summed = jnp.sum(samples, axis=0)  20.3 us
    all_to_all x4, starting transfers between devices, shards(): lax.all_to_all(pieces, 'tile', split_axis=0, concat_axis=0, tiled=True)  15.8 us
    all_to_all x2, blocking collectives, shards(): lax.all_to_all(edges, 'tile', split_axis=0, concat_axis=0, tiled=True)  15.7 us
    reshape x4, local copies, waits for them, and re-layouts, interpolate(): first = jnp.repeat(first, 4, axis=-1)  14.7 us
  transfers between devices with their start and end apart: 14, of which 2 were waited for; matrix products, arithmetic and copies ran while one was open for 24% of the time, Pallas kernels for 0%

profile of v1, /device:TPU:0, one launch (start us, length us, event | category | flops | bytes accessed | tf_op | source)
XLA Modules:
  0.0 443.3 jit_solution(14845577191541846631)
XLA Ops:
  21.7 11.0 %while.17 = (s32[]{:T(128)}, bf16[1,2,2048]{2,1,0:T(2,128)(2,1)S(1)}, s32[8,3]{0,1:T(4,128)S(1)}, bf16[8,2,1025]{2,1,0:T(2,128)(2,1)S(1)}, s32[]{:T(128)}) while((s32[]{:T(128)}, bf16[1,2,2048]{2,1,0:T(2,128)(2,1)S(1)}, s32[8,3]{0,1:T(4,128)S(1)}, bf16[8,2,1025]{2,1,0:T(2,128)(2,1)S(1)}, s32[]{:T(128)}) %tuple.191), condition=%wide.while_cond.13, body=%wide.while_body.13.sunk | while | flops 2 | bytes 9321 | solution.py:37
  33.5 5.2 %all-to-all-start.7 = ((bf16[8,1,2]{2,1,0:T(2,128)(2,1)}), bf16[8,1,2]{2,1,0:T(2,128)(2,1)S(1)}, u32[]{:S(2)}, u32[]{:S(2)}) async-start(bf16[8,1,2]{2,1,0:T(2,128)(2,1)} %copy.117), calls=%async_computation.7 | async-start | bytes 8192 | tf_op jit(solution)/shard_map/all_to_all | solution.py:95
  39.3 42.3 %all-gather.4 = s32[32,1,4]{2,1,0:T(1,128)S(1)} all-gather(s32[1,1,4]{2,1,0:T(1,128)S(1)} %bitcast.332), channel_id=1, replica_groups=mesh['pulse'=4,'tile'=8] {'pulse','tile'}, dimensions={0}, use_global_device_ids=true | all-gather | bytes 528 | tf_op jit(solution)/shard_map/all_gather | solution.py:71
  82.2 37.3 %all-reduce.6 = (s32[128]{0:T(128)S(1)}, s32[128]{0:T(128)S(1)}) all-reduce(s32[128]{0:T(128)S(1)} %dynamic-update-slice.19, s32[128]{0:T(128)S(1)} %dynamic-update-slice.18), channel_id=1, replica_groups=mesh['pulse'=4,'tile'=8] {'pulse','tile'}, use_global_device_ids=true, to_apply=%add.5 | all-reduce | flops 256 | bytes 2048
  136.7 11.0 %while.16 = (s32[]{:T(128)}, bf16[1,2,2048]{2,1,0:T(2,128)(2,1)S(1)}, s32[8,3]{0,1:T(4,128)S(1)}, bf16[8,2,1025]{2,1,0:T(2,128)(2,1)S(1)}, s32[]{:T(128)}) while((s32[]{:T(128)}, bf16[1,2,2048]{2,1,0:T(2,128)(2,1)S(1)}, s32[8,3]{0,1:T(4,128)S(1)}, bf16[8,2,1025]{2,1,0:T(2,128)(2,1)S(1)}, s32[]{:T(128)}) %tuple.188), condition=%wide.while_cond.10, body=%wide.while_body.10.sunk | while | flops 2 | bytes 9321 | solution.py:37
  159.8 11.5 %while.15 = (s32[]{:T(128)}, bf16[1,2,2048]{2,1,0:T(2,128)(2,1)S(1)}, s32[8,3]{0,1:T(4,128)S(1)}, bf16[8,2,1025]{2,1,0:T(2,128)(2,1)S(1)}, s32[]{:T(128)}) while((s32[]{:T(128)}, bf16[1,2,2048]{2,1,0:T(2,128)(2,1)S(1)}, s32[8,3]{0,1:T(4,128)S(1)}, bf16[8,2,1025]{2,1,0:T(2,128)(2,1)S(1)}, s32[]{:T(128)}) %tuple.185), condition=%wide.while_cond.7, body=%wide.while_body.7.sunk | while | flops 2 | bytes 9321 | solution.py:37
  183.5 10.6 %while.14 = (s32[]{:T(128)}, bf16[1,2,2048]{2,1,0:T(2,128)(2,1)S(1)}, s32[8,3]{0,1:T(4,128)S(1)}, bf16[8,2,1025]{2,1,0:T(2,128)(2,1)S(1)}, s32[]{:T(128)}) while((s32[]{:T(128)}, bf16[1,2,2048]{2,1,0:T(2,128)(2,1)S(1)}, s32[8,3]{0,1:T(4,128)S(1)}, bf16[8,2,1025]{2,1,0:T(2,128)(2,1)S(1)}, s32[]{:T(128)}) %tuple.182), condition=%wide.while_cond.4, body=%wide.while_body.4.sunk | while | flops 2 | bytes 9321 | solution.py:37
  222.1 13.8 %all-gather.3 = bf16[32,1,2]{2,1,0:T(2,128)(2,1)S(1)} all-gather(bf16[8,1,2]{2,1,0:T(2,128)(2,1)S(1)} %all-to-all-done.7), channel_id=5, replica_groups=mesh['pulse'=4,'tile'=8] {'pulse'}, dimensions={0}, use_global_device_ids=true | all-gather | bytes 160 | tf_op jit(solution)/shard_map/all_gather | solution.py:99
  235.9 8.7 %all_to_all.68 = bf16[8,1,2]{2,1,0:T(2,128)(2,1)S(1)} all-to-all(bf16[8,1,2]{2,1,0:T(2,128)(2,1)S(1)} %copy.97), channel_id=1, replica_groups=mesh['pulse'=4,'tile'=8] {'tile'}, dimensions={0} | all-to-all | bytes 64 | tf_op jit(solution)/shard_map/all_to_all | solution.py:95
  244.6 7.0 %all_to_all.69 = bf16[8,1,2]{2,1,0:T(2,128)(2,1)S(1)} all-to-all(bf16[8,1,2]{2,1,0:T(2,128)(2,1)S(1)} %copy.87), channel_id=1, replica_groups=mesh['pulse'=4,'tile'=8] {'tile'}, dimensions={0} | all-to-all | bytes 64 | tf_op jit(solution)/shard_map/all_to_all | solution.py:95
  255.0 13.2 %all-gather.2 = bf16[32,1,2]{2,1,0:T(2,128)(2,1)S(1)} all-gather(bf16[8,1,2]{2,1,0:T(2,128)(2,1)S(1)} %all-to-all-done.5), channel_id=4, replica_groups=mesh['pulse'=4,'tile'=8] {'pulse'}, dimensions={0}, use_global_device_ids=true | all-gather | bytes 160 | tf_op jit(solution)/shard_map/all_gather | solution.py:99
  268.3 4.1 all-to-all-start.4
  272.4 13.2 %all-gather.1 = bf16[32,1,2]{2,1,0:T(2,128)(2,1)S(1)} all-gather(bf16[8,1,2]{2,1,0:T(2,128)(2,1)S(1)} %all_to_all.68), channel_id=3, replica_groups=mesh['pulse'=4,'tile'=8] {'pulse'}, dimensions={0}, use_global_device_ids=true | all-gather | bytes 160 | tf_op jit(solution)/shard_map/all_gather | solution.py:99
  285.7 4.2 all-to-all-start.2
  289.9 13.2 %all-gather = bf16[32,1,2]{2,1,0:T(2,128)(2,1)S(1)} all-gather(bf16[8,1,2]{2,1,0:T(2,128)(2,1)S(1)} %all_to_all.69), channel_id=2, replica_groups=mesh['pulse'=4,'tile'=8] {'pulse'}, dimensions={0}, use_global_device_ids=true | all-gather | bytes 160 | tf_op jit(solution)/shard_map/all_gather | solution.py:99
  303.7 4.2 all-to-all-start
  334.7 3.9 broadcast_in_dim.162
  338.6 3.6 copy.121
  342.2 3.9 broadcast_in_dim.159
  346.1 3.6 copy.115
  349.7 5.3 %add_reduce_fusion = f32[2,1024,4]{2,1,0:T(8,128)S(1)} fusion(f32[32,1024,4]{0,2,1:T(4,128)} %copy.123, f32[32,1024,4]{0,2,1:T(4,128)} %copy.122, f32[32,2,1024]{0,2,1:T(8,128)} %copy.120, f32[32,2,1024]{0,2,1:T(8,128)} %copy.114), kind=kLoop, calls=%fused_computation.52 | loop fusion | flops 1040384 | bytes 1605632 | tf_op jit(solution)/shard_map/reduce_sum | solution.py:103
  361.1 3.9 broadcast_in_dim.155
  365.0 3.6 copy.111
  371.3 3.8 copy.105
  375.1 5.1 %add_reduce_fusion.1 = f32[2,1024,4]{2,1,0:T(8,128)S(1)} fusion(f32[32,1024,4]{0,2,1:T(4,128)} %copy.113, f32[32,1024,4]{0,2,1:T(4,128)} %copy.112, f32[32,2,1024]{0,2,1:T(8,128)} %copy.110, f32[32,2,1024]{0,2,1:T(8,128)S(1)} %copy.104), kind=kLoop, calls=%fused_computation.53 | loop fusion | flops 1040384 | bytes 1605632 | tf_op jit(solution)/shard_map/reduce_sum | solution.py:103
  385.0 3.6 copy.101
  391.3 3.6 copy.95
  394.9 5.0 %add_reduce_fusion.2 = f32[2,1024,4]{2,1,0:T(8,128)S(1)} fusion(f32[32,1024,4]{0,2,1:T(4,128)} %copy.103, f32[32,1024,4]{0,2,1:T(4,128)} %copy.102, f32[32,2,1024]{0,2,1:T(8,128)S(1)} %copy.100, f32[32,2,1024]{0,2,1:T(8,128)S(1)} %copy.94), kind=kLoop, calls=%fused_computation.54 | loop fusion | flops 1040384 | bytes 1605632 | tf_op jit(solution)/shard_map/reduce_sum | solution.py:103
  401.0 5.0 %add_reduce_fusion.3 = f32[2,1024,4]{2,1,0:T(8,128)S(1)} fusion(f32[32,1024,4]{0,2,1:T(4,128)} %copy.93, f32[32,1024,4]{0,2,1:T(4,128)} %copy.92, f32[32,2,1024]{0,2,1:T(8,128)S(1)} %copy.90, f32[32,2,1024]{0,2,1:T(8,128)S(1)} %copy.84), kind=kLoop, calls=%fused_computation.55 | loop fusion | flops 1040384 | bytes 1605632 | tf_op jit(solution)/shard_map/reduce_sum | solution.py:103
  409.3 3.8 copy.91
  415.9 3.7 copy.85
  424.8 11.8 %all-reduce.7 = (f32[32]{0:T(128)S(1)}, f32[32]{0:T(128)S(1)}, f32[32]{0:T(128)S(1)}, f32[32]{0:T(128)S(1)}, f32[32]{0:T(128)S(1)}, /*index=5*/f32[32]{0:T(128)S(1)}, f32[32]{0:T(128)S(1)}, f32[32]{0:T(128)S(1)}) all-reduce(f32[32]{0:T(128)S(1)} %get-tuple-element.157, ...), channel_id=1, replica_groups=mesh['pulse'=4,'tile'=8] {'tile'}, use_global_device_ids=true, to_apply=%region_4.8 | all-reduce | flops 256 | bytes 2048 | tf_op jit(solution)/shard_map/psum | solution.py:105
  (352 shorter events, 192.4 us)
Async XLA Ops:
  13.9 6.3 %copy-start = (bf16[2,1024,2048]{2,1,0:T(8,128)(2,1)S(1)}, bf16[2,1024,2048]{2,1,0:T(8,128)(2,1)}, u32[]{:S(2)}) copy-start(bf16[2,1024,2048]{2,1,0:T(8,128)(2,1)} %param.14) | copy-start | bytes 25165828
  20.2 19.1 %copy-start.24 = (s32[1,4]{1,0:T(1,128)S(1)}, s32[1,4]{1,0:T(1,128)}, u32[]{:S(2)}) copy-start(s32[1,4]{1,0:T(1,128)} %param.18) | copy-start | bytes 52
  20.2 61.5 %copy-start.26 = (s32[4]{0:T(128)S(1)}, s32[4]{0:T(128)}, u32[]{:S(2)}) copy-start(s32[4]{0:T(128)} %param.17) | copy-start | bytes 52
  20.2 61.7 %copy-start.27 = (s32[4]{0:T(128)S(1)}, s32[4]{0:T(128)}, u32[]{:S(2)}) copy-start(s32[4]{0:T(128)} %param.16) | copy-start | bytes 52
  33.5 185.0 %all-to-all-start.7 = ((bf16[8,1,2]{2,1,0:T(2,128)(2,1)}), bf16[8,1,2]{2,1,0:T(2,128)(2,1)S(1)}, u32[]{:S(2)}, u32[]{:S(2)}) async-start(bf16[8,1,2]{2,1,0:T(2,128)(2,1)} %copy.117), calls=%async_computation.7 | async-start | bytes 8192 | tf_op jit(solution)/shard_map/all_to_all | solution.py:95
  218.5 17.4 %all-to-all-start.5 = ((bf16[8,1,2]{2,1,0:T(2,128)(2,1)}), bf16[8,1,2]{2,1,0:T(2,128)(2,1)S(1)}, u32[]{:S(2)}, u32[]{:S(2)}) async-start(bf16[8,1,2]{2,1,0:T(2,128)(2,1)} %copy.107), calls=%async_computation.5 | async-start | bytes 8192 | tf_op jit(solution)/shard_map/all_to_all | solution.py:95
  251.7 16.7 %all-to-all-start.6 = ((bf16[8,2,1024]{2,1,0:T(2,128)(2,1)}), bf16[8,2,1024]{2,1,0:T(2,128)(2,1)S(1)}, u32[]{:S(2)}, u32[]{:S(2)}) async-start(bf16[8,2,1024]{2,1,0:T(2,128)(2,1)} %slice_bitcast_fusion.8), calls=%async_computation.6 | async-start | bytes 65536 | tf_op jit(solution)/shard_map/all_to_all | solution.py:94
  268.3 17.4 %all-to-all-start.4 = ((bf16[8,2,1024]{2,1,0:T(2,128)(2,1)}), bf16[8,2,1024]{2,1,0:T(2,128)(2,1)S(1)}, u32[]{:S(2)}, u32[]{:S(2)}) async-start(bf16[8,2,1024]{2,1,0:T(2,128)(2,1)} %slice_bitcast_fusion.9), calls=%async_computation.4 | async-start | bytes 65536 | tf_op jit(solution)/shard_map/all_to_all | solution.py:94
  285.7 18.0 %all-to-all-start.2 = ((bf16[8,2,1024]{2,1,0:T(2,128)(2,1)}), bf16[8,2,1024]{2,1,0:T(2,128)(2,1)S(1)}, u32[]{:S(2)}, u32[]{:S(2)}) async-start(bf16[8,2,1024]{2,1,0:T(2,128)(2,1)} %slice_bitcast_fusion.10), calls=%async_computation.2 | async-start | bytes 65536 | tf_op jit(solution)/shard_map/all_to_all | solution.py:94
  303.2 11.1 %collective-permute-start.6 = (bf16[8,2,1024]{2,1,0:T(2,128)(2,1)S(1)}, bf16[8,2,1024]{2,1,0:T(2,128)(2,1)S(1)}, u32[]{:S(2)}, u32[]{:S(2)}) collective-permute-start(bf16[8,2,1024]{2,1,0:T(2,128)(2,1)S(1)} %all-to-all-done.6), channel_id=1, source_target_pairs={{0,8},{8,0},{16,24},{24,16},{1,9},{9,1},{17,25},{25,17},{2,10},{10... | collective-permute-start | bytes 98312 | tf_op jit(solution)/shard_map/ppermute | solution.py:16
  303.7 9.0 %all-to-all-start = ((bf16[8,2,1024]{2,1,0:T(2,128)(2,1)}), bf16[8,2,1024]{2,1,0:T(2,128)(2,1)S(1)}, u32[]{:S(2)}, u32[]{:S(2)}) async-start(bf16[8,2,1024]{2,1,0:T(2,128)(2,1)} %slice_bitcast_fusion.11), calls=%async_computation | async-start | bytes 65536 | tf_op jit(solution)/shard_map/all_to_all | solution.py:94
  308.3 7.0 %collective-permute-start.4 = (bf16[8,2,1024]{2,1,0:T(2,128)(2,1)S(1)}, bf16[8,2,1024]{2,1,0:T(2,128)(2,1)S(1)}, u32[]{:S(2)}, u32[]{:S(2)}) collective-permute-start(bf16[8,2,1024]{2,1,0:T(2,128)(2,1)S(1)} %all-to-all-done.4), channel_id=1, source_target_pairs={{0,8},{8,0},{16,24},{24,16},{1,9},{9,1},{17,25},{25,17},{2,10},{10... | collective-permute-start | bytes 98312 | tf_op jit(solution)/shard_map/ppermute | solution.py:16
  309.9 7.7 %collective-permute-start.2 = (bf16[8,2,1024]{2,1,0:T(2,128)(2,1)S(1)}, bf16[8,2,1024]{2,1,0:T(2,128)(2,1)S(1)}, u32[]{:S(2)}, u32[]{:S(2)}) collective-permute-start(bf16[8,2,1024]{2,1,0:T(2,128)(2,1)S(1)} %all-to-all-done.2), channel_id=1, source_target_pairs={{0,8},{8,0},{16,24},{24,16},{1,9},{9,1},{17,25},{25,17},{2,10},{10... | collective-permute-start | bytes 98312 | tf_op jit(solution)/shard_map/ppermute | solution.py:16
  312.8 6.0 %collective-permute-start = (bf16[8,2,1024]{2,1,0:T(2,128)(2,1)S(1)}, bf16[8,2,1024]{2,1,0:T(2,128)(2,1)S(1)}, u32[]{:S(2)}, u32[]{:S(2)}) collective-permute-start(bf16[8,2,1024]{2,1,0:T(2,128)(2,1)S(1)} %all-to-all-done), channel_id=1, source_target_pairs={{0,8},{8,0},{16,24},{24,16},{1,9},{9,1},{17,25},{25,17},{2,10},{10... | collective-permute-start | bytes 98312 | tf_op jit(solution)/shard_map/ppermute | solution.py:16
  314.5 10.1 %collective-permute-start.7 = (bf16[16,2,1024]{2,1,0:T(2,128)(2,1)S(1)}, bf16[16,2,1024]{2,1,0:T(2,128)(2,1)S(1)}, u32[]{:S(2)}, u32[]{:S(2)}) collective-permute-start(bf16[16,2,1024]{2,1,0:T(2,128)(2,1)S(1)} %broadcast_select_fusion.4), channel_id=1, source_target_pairs={{0,16},{8,24},{16,0},{24,8},{1,17},{9,25},{17,1},{25,9},{2,18},{10... | collective-permute-start | bytes 196616 | tf_op jit(solution)/shard_map/ppermute | solution.py:16
  315.5 11.7 %collective-permute-start.5 = (bf16[16,2,1024]{2,1,0:T(2,128)(2,1)S(1)}, bf16[16,2,1024]{2,1,0:T(2,128)(2,1)S(1)}, u32[]{:S(2)}, u32[]{:S(2)}) collective-permute-start(bf16[16,2,1024]{2,1,0:T(2,128)(2,1)S(1)} %broadcast_select_fusion.5), channel_id=1, source_target_pairs={{0,16},{8,24},{16,0},{24,8},{1,17},{9,25},{17,1},{25,9},{2,18},{10... | collective-permute-start | bytes 196616 | tf_op jit(solution)/shard_map/ppermute | solution.py:16
  317.8 11.1 %collective-permute-start.3 = (bf16[16,2,1024]{2,1,0:T(2,128)(2,1)S(1)}, bf16[16,2,1024]{2,1,0:T(2,128)(2,1)S(1)}, u32[]{:S(2)}, u32[]{:S(2)}) collective-permute-start(bf16[16,2,1024]{2,1,0:T(2,128)(2,1)S(1)} %broadcast_select_fusion.6), channel_id=1, source_target_pairs={{0,16},{8,24},{16,0},{24,8},{1,17},{9,25},{17,1},{25,9},{2,18},{10... | collective-permute-start | bytes 196616 | tf_op jit(solution)/shard_map/ppermute | solution.py:16
  318.9 11.7 %collective-permute-start.1 = (bf16[16,2,1024]{2,1,0:T(2,128)(2,1)S(1)}, bf16[16,2,1024]{2,1,0:T(2,128)(2,1)S(1)}, u32[]{:S(2)}, u32[]{:S(2)}) collective-permute-start(bf16[16,2,1024]{2,1,0:T(2,128)(2,1)S(1)} %broadcast_select_fusion.7), channel_id=1, source_target_pairs={{0,16},{8,24},{16,0},{24,8},{1,17},{9,25},{17,1},{25,9},{2,18},{10... | collective-permute-start | bytes 196616 | tf_op jit(solution)/shard_map/ppermute | solution.py:16
  394.9 5.6 %copy-start.16 = (f32[32,2,1023]{2,1,0:T(2,128)S(1)}, f32[32,2,1023]{2,1,0:T(2,128)}, u32[]{:S(2)}) copy-start(f32[32,2,1023]{2,1,0:T(2,128)} %slice.397) | copy-start | bytes 785668
  413.2 6.4 %copy-start.2 = (f32[32,2,4096]{2,0,1:T(8,128)S(1)}, f32[32,2,4096]{2,0,1:T(8,128)}, u32[]{:S(2)}) copy-start(f32[32,2,4096]{2,0,1:T(8,128)} %copy.121) | copy-start | bytes 3145732
  413.2 6.4 %copy-start.3 = (f32[32,2,4096]{2,0,1:T(8,128)S(1)}, f32[32,2,4096]{2,0,1:T(8,128)}, u32[]{:S(2)}) copy-start(f32[32,2,4096]{2,0,1:T(8,128)} %copy.115) | copy-start | bytes 3145732
  415.9 5.6 %copy-start.4 = (f32[32,2,4096]{2,0,1:T(8,128)S(1)}, f32[32,2,4096]{2,0,1:T(8,128)}, u32[]{:S(2)}) copy-start(f32[32,2,4096]{2,0,1:T(8,128)} %copy.111) | copy-start | bytes 3145732
  421.1 2.4 copy-start.1
  421.1 2.0 copy-start.7
  421.1 2.1 copy-start.12
  421.1 2.2 copy-start.13
  421.7 2.1 copy-start.8
  421.7 2.3 copy-start.9
  421.7 2.4 copy-start.10
  421.7 2.6 copy-start.11
  424.5 14.2 %copy-start.22 = (bf16[1,64,128]{2,1,0:T(8,128)(2,1)S(1)}, bf16[1,64,128]{2,1,0:T(8,128)(2,1)}, u32[]{:S(2)}) copy-start(bf16[1,64,128]{2,1,0:T(8,128)(2,1)} %get-tuple-element.254) | copy-start | bytes 49156
  424.5 14.2 %copy-start.23 = (bf16[1,64,128]{2,1,0:T(8,128)(2,1)S(1)}, bf16[1,64,128]{2,1,0:T(8,128)(2,1)}, u32[]{:S(2)}) copy-start(bf16[1,64,128]{2,1,0:T(8,128)(2,1)} %get-tuple-element.255) | copy-start | bytes 49156
  (10 other events, 13.4 us)
